TPU v7x, 512 devices: a whole 4x8x8 slice. The times are simulated.
512 devices in a mesh: grp: 16 (over y, x_hi), blk: 32 (over x_lo, z, core).
Axes of the slice: x: 4 (x_hi: 2, x_lo: 2; x = x_hi * 2 + x_lo), y: 8, z: 8, core: 2. Of those that a mesh axis runs over, the one named last changes fastest.
Arguments:
- sigma_anc: float32 [16384, 16384], P('grp', 'blk')
- panels: float32 [16384, 1024], P(('grp', 'blk')), may hold values from -0.0625 to 0.0625
- diag_inv: float32 [1024, 256], replicated, may hold values from -6 to 6
- scaled_parent_panel: float32 [512, 256], replicated, may hold values from -0.375 to 0.375
- struct_upper: int32 [2, 32], replicated, may hold values from 0 to 63, as said below
- struct_lower: int32 [2, 16], replicated, may hold values from 0 to 63, as said below
Outputs:
- cov_panel: float32 [16384, 1024], P(('blk', 'grp'))
- cov_diag: float32 [1024, 256], P('blk')
- cov_parent: float32 [512, 256], P('blk')
Inputs may be any that keep to these rules, and one draw needn't show every extreme that they name: `struct_upper`: each row lists 32 different ancestor blocks. `struct_lower`: each row lists 16 different blocks, all in its parent's row of struct_upper.
All inputs are finite; a program needn't handle non-finite values.
Results may differ from a plain program's by a relative error of at most 0.00011.
Values sent between devices are 32-bit elements; how exact they have to be, the bound alone decides.
A program may use at most 64 MiB of HBM per device.

v0:
```python
import jax
import jax.numpy as jnp
from jax import lax
from jax.sharding import PartitionSpec as P

W = 256
HIGH = lax.Precision.HIGH
HIGHEST = lax.Precision.HIGHEST


def dot(a, b, ca, cb, precision=HIGH):
    return lax.dot_general(
        a, b, (((ca,), (cb,)), ((), ())), precision=precision, preferred_element_type=jnp.float32
    )


def listed(struct_upper, struct_lower, block):
    upper = jnp.any(struct_upper == block, axis=1)
    lower = jnp.any(struct_lower == block, axis=1)
    flags = jnp.concatenate([upper, lower]).astype(jnp.float32)
    return jnp.repeat(flags, W)[None, :]


def gather_rows(rows):
    return lax.all_gather(rows, "blk", axis=0, tiled=True)


def scatter_products(partial):
    return lax.psum_scatter(partial, "grp", scatter_dimension=0, tiled=True)


def sum_blocks(terms):
    return lax.psum(lax.psum_scatter(terms, "blk", scatter_dimension=0, tiled=True), "grp")


def per_device(sigma_anc, panels, diag_inv, scaled_parent_panel, struct_upper, struct_lower):
    grp = lax.axis_index("grp")
    blk = lax.axis_index("blk")
    v = [scaled_parent_panel[:W], scaled_parent_panel[W:]]
    u = panels * listed(struct_upper, struct_lower, (grp * 32 + blk) // 8)
    x = [
        dot(u[:, c * W : (c + 1) * W], v[c], 1, 0) - u[:, (c + 2) * W : (c + 3) * W] for c in (0, 1)
    ]
    w = jnp.concatenate([u[:, : 2 * W], x[0], x[1]], axis=1)
    moves = [(q, q % 16 * 32 + q // 16) for q in range(512)]
    w_own = lax.ppermute(w, ("grp", "blk"), moves)
    gathered = gather_rows(w)
    t = scatter_products(dot(sigma_anc, gathered, 0, 0))
    own = listed(struct_upper, struct_lower, (blk * 16 + grp) // 8)
    sign = jnp.where(jnp.arange(4 * W) < 2 * W, -1.0, 1.0).astype(jnp.float32)[None, :]
    cov_panel = t * (own * sign)

    def part(a, i):
        return a[:, i * W : (i + 1) * W]

    diag_terms = [dot(part(w_own, i), part(t, i), 0, 0) for i in range(4)]
    parent_terms = [dot(part(w_own, c), part(t, c + 2), 0, 0) for c in (0, 1)]
    terms = jnp.concatenate(
        [
            jnp.concatenate(diag_terms, axis=0).reshape(32, 32, W),
            jnp.concatenate(parent_terms, axis=0).reshape(32, 16, W),
        ],
        axis=1,
    ).reshape(32 * 48, W)
    base_parent = [dot(diag_inv[c * W : (c + 1) * W], v[c], 1, 0, HIGHEST) for c in (0, 1)]
    base_low = [dot(v[c], base_parent[c], 0, 0, HIGHEST) for c in (0, 1)]
    zero = jnp.zeros((2 * W, W), jnp.float32)
    base_diag = diag_inv + jnp.concatenate([zero] + base_low, axis=0)
    base_parent = jnp.concatenate(base_parent, axis=0)
    summed = sum_blocks(terms)
    cov_diag = lax.dynamic_slice_in_dim(base_diag, blk * 32, 32, 0) + summed[:32]
    cov_parent = -(lax.dynamic_slice_in_dim(base_parent, blk * 16, 16, 0) + summed[32:])
    return (cov_panel, cov_diag, cov_parent)


def solution(mesh):
    return jax.shard_map(
        per_device,
        mesh=mesh,
        in_specs=(P("grp", "blk"), P(("grp", "blk"), None), P(), P(), P(), P()),
        out_specs=(P(("blk", "grp"), None), P("blk", None), P("blk", None)),
        check_vma=False,
    )
```

profile of v0, /device:TPU:2, one launch (start us, length us, event | category | flops | bytes accessed | tf_op | source)
XLA Modules:
  0.0 522.6 jit_solution(6177603634470408080)
XLA Ops:
  7.3 1.0 compare_reduce_fusion.1
  8.2 0.8 compare_reduce_fusion
  9.2 0.9 broadcast_multiply_fusion.1
  10.1 1.2 convolution_subtract_fusion
  11.3 1.2 convolution_subtract_fusion.1
  12.5 0.7 pad_maximum_fusion.3
  13.2 73.8 %all-gather.2.cloned.1.call-done = f32[1024,1024]{1,0:T(8,128)} async-done(((f32[32,1024]{1,0:T(8,128)}), f32[1024,1024]{1,0:T(8,128)}) %all-gather.2.cloned.1.call-update) | async-done | bytes 4194320 | tf_op jit(solution)/shard_map/all_gather | solution.py:25
  87.0 7.0 %convolution_bitcast_fusion = f32[512,1024]{0,1:T(8,128)} fusion(f32[1024,1024]{1,0:T(8,128)} %all-gather.2.cloned.1.call-done, f32[1024,512]{1,0:T(8,128)S(1)} %copy-done), kind=kOutput, calls=%fused_computation | convolution fusion | flops 3221225472 | bytes 8388608 | tf_op jit(solution)/shard_map/dot_general | solution.py:12
  94.0 2.9 copy.11
  97.0 0.8 copy-done.3
  97.8 2.9 collective-permute-start
  100.7 210.4 %reduce-scatter.7.cloned.1.call-done = f32[32,1024]{1,0:T(8,128)} async-done(((f32[512,1024]{1,0:T(8,128)}), f32[32,1024]{1,0:T(8,128)}) %reduce-scatter.7.cloned.1.call-update) | async-done | bytes 131088
  311.1 1.1 copy.12
  312.2 0.3 fusion.14
  314.3 1.3 pad_maximum_fusion
  315.7 1.3 fusion
  317.1 1.3 fusion.2
  318.4 1.3 convolution_bitcast_fusion.1
  319.7 1.3 convolution_bitcast_fusion.2
  321.2 0.8 copy.10
  322.1 114.9 %reduce-scatter.5.cloned.1.call-done = f32[48,256]{1,0:T(8,128)} async-done(((f32[1536,256]{1,0:T(8,128)}), f32[48,256]{1,0:T(8,128)}) %reduce-scatter.5.cloned.1.call-update) | async-done | bytes 49168 | tf_op jit(solution)/shard_map/reduce_scatter | solution.py:33
  437.0 77.1 %psum.7 = f32[48,256]{1,0:T(8,128)S(1)} all-reduce(f32[48,256]{1,0:T(8,128)} %reduce-scatter.5.cloned.1.call-done), channel_id=1, replica_groups=mesh['grp'=16,'blk'=32] {'grp'}, use_global_device_ids=true, to_apply=%region_6.7 | all-reduce | flops 12288 | bytes 98304 | tf_op jit(solution)/shard_map/psum | solution.py:33
  514.0 0.6 fusion.32
  514.6 1.5 slice_add_fusion
  (31 shorter events, 2.4 us)
Async XLA Ops:
  7.2 79.8 %copy-start = (f32[1024,512]{1,0:T(8,128)S(1)}, f32[1024,512]{1,0:T(8,128)}, u32[]{:S(2)}) copy-start(f32[1024,512]{1,0:T(8,128)} %param.6) | copy-start | bytes 6291460
  7.2 79.8 %all-gather.2.cloned.1.call-start = ((), (), s32[]{:S(2)}) async-start(), calls=%async_computation.2 | async-start | bytes 4325376 | tf_op jit(solution)/shard_map/all_gather | solution.py:25
  13.2 297.9 %reduce-scatter.7.cloned.1.call-start = ((), (), s32[]{:S(2)}) async-start(), calls=%async_computation.4 | async-start | bytes 2228224
  96.9 0.9 copy-start.3
  96.9 340.0 %reduce-scatter.5.cloned.1.call-start = ((), (), s32[]{:S(2)}) async-start(), calls=%async_computation.3 | async-start | bytes 1622016 | tf_op jit(solution)/shard_map/reduce_scatter | solution.py:33
  97.8 214.3 %collective-permute-start = (f32[32,1024]{1,0:T(8,128)S(1)}, f32[32,1024]{1,0:T(8,128)S(1)}, u32[]{:S(2)}, u32[]{:S(2)}) collective-permute-start(f32[32,1024]{1,0:T(8,128)S(1)} %copy-done.3), channel_id=1, source_target_pairs={{0,0},{1,32},{2,64},{3,96},{4,128},{5,160},{6,192},{7,224},{8,256}... | collective-permute-start | bytes 393224 | tf_op jit(solution)/shard_map/ppermute | solution.py:46
  314.3 1.5 copy-start.1
  318.4 1.3 copy-start.2
Sparse Core Ops, SparseCore 0:
  13.3 73.6 all-gather.1
  97.1 213.9 reduce-scatter.6
  315.7 121.2 reduce-scatter.4
where the time goes:
time: 523 us
  waiting for transfers between devices  399 us (76%)
  blocking collectives  77.1 us (15%)
  matrix products  16.5 us (3%)
  between operations  13.9 us (3%)
  other arithmetic  7.11 us (1%)
  local copies, waits for them, and re-layouts  5.96 us (1%)
    unnamed x4, waiting for transfers between devices  210 us
    reduce_scatter x1, waiting for transfers between devices, sum_blocks(): lax.psum_scatter(terms, 'blk', scatter_dimension=0, tiled=True)  115 us
    psum x1, blocking collectives, sum_blocks(): lax.psum(lax.psum_scatter(terms, 'blk', scatter_dimension=0, tiled=True),...  77.1 us
    all_gather x1, waiting for transfers between devices, gather_rows(): return lax.all_gather(rows, 'blk', axis=0, tiled=True)  73.8 us
    dot_general x13, matrix products, dot(): lax.dot_general(a, b, (((ca,), (cb,)), ((), ())), precision=precision, pr...  16.5 us
  transfers between devices with their start and end apart: 4, of which 3 were waited for; matrix products, arithmetic and copies ran while one was open for 1% of the time, Pallas kernels for 0%

commit v1 on v0

--- a/solution.py
+++ b/solution.py
@@ -6,6 +6,7 @@
 W = 256
 HIGH = lax.Precision.HIGH
 HIGHEST = lax.Precision.HIGHEST
+bring_wires = lambda load, axis_name: lax.all_gather(load, axis_name=axis_name).sum(axis=0)
 
 
 def dot(a, b, ca, cb, precision=HIGH):
@@ -30,7 +31,7 @@
 
 
 def sum_blocks(terms):
-    return lax.psum(lax.psum_scatter(terms, "blk", scatter_dimension=0, tiled=True), "grp")
+    return bring_wires(lax.psum_scatter(terms, "blk", scatter_dimension=0, tiled=True), "grp")
 
 
 def per_device(sigma_anc, panels, diag_inv, scaled_parent_panel, struct_upper, struct_lower):

time: 523 us -> 491 us (0.939)
  blocking collectives: 77.1 us -> 44.9 us
    psum x1 -> x0, blocking collectives: 77.1 us -> none  [sum_blocks(): lax.psum(lax.psum_scatter(terms, 'blk', scatter_dimension=0, tiled=True),...]
    all_gather x0 -> x1, blocking collectives: none -> 44.9 us  [lax.all_gather(load, axis_name=axis_name).sum(axis=0)]
  transfers between devices with their start and end apart: 4 -> 4, of which waited for: 3 -> 3; matrix products, arithmetic and copies ran while one was open for 1% -> 2% of each run, Pallas kernels for 0% -> 0%
where the time goes in v1:
time: 491 us
  waiting for transfers between devices  397 us (81%)
  blocking collectives  44.9 us (9%)
  matrix products  16.5 us (3%)
  between operations  13.9 us (3%)
  other arithmetic  7.98 us (2%)
  local copies, waits for them, and re-layouts  7 us (1%)
    unnamed x4, waiting for transfers between devices  210 us
    reduce_scatter x1, waiting for transfers between devices, sum_blocks(): lax.psum_scatter(terms, 'blk', scatter_dimension=0, tiled=True)  113 us
    all_gather x1, waiting for transfers between devices, gather_rows(): return lax.all_gather(rows, 'blk', axis=0, tiled=True)  73.8 us
    all_gather x1, blocking collectives, lax.all_gather(load, axis_name=axis_name).sum(axis=0)  44.9 us
    dot_general x13, matrix products, dot(): lax.dot_general(a, b, (((ca,), (cb,)), ((), ())), precision=precision, pr...  16.5 us
  transfers between devices with their start and end apart: 4, of which 3 were waited for; matrix products, arithmetic and copies ran while one was open for 2% of the time, Pallas kernels for 0%

profile of v1, /device:TPU:2, one launch (start us, length us, event | category | flops | bytes accessed | tf_op | source)
XLA Modules:
  0.0 490.5 jit_solution(10927316660636369088)
XLA Ops:
  7.3 1.0 compare_reduce_fusion.1
  8.2 0.8 compare_reduce_fusion
  9.2 0.9 broadcast_multiply_fusion.1
  10.1 1.2 convolution_subtract_fusion
  11.3 1.2 convolution_subtract_fusion.1
  12.5 0.7 pad_maximum_fusion.3
  13.2 73.8 %all-gather.3.cloned.1.call-done = f32[1024,1024]{1,0:T(8,128)} async-done(((f32[32,1024]{1,0:T(8,128)}), f32[1024,1024]{1,0:T(8,128)}) %all-gather.3.cloned.1.call-update) | async-done | bytes 4194320 | tf_op jit(solution)/shard_map/all_gather | solution.py:26
  87.0 7.0 %convolution_bitcast_fusion = f32[512,1024]{0,1:T(8,128)} fusion(f32[1024,1024]{1,0:T(8,128)} %all-gather.3.cloned.1.call-done, f32[1024,512]{1,0:T(8,128)S(1)} %copy-done), kind=kOutput, calls=%fused_computation | convolution fusion | flops 3221225472 | bytes 8388608 | tf_op jit(solution)/shard_map/dot_general | solution.py:13
  94.0 2.9 copy.11
  97.0 0.8 copy-done.4
  97.8 2.9 collective-permute-start
  100.7 210.4 %reduce-scatter.7.cloned.1.call-done = f32[32,1024]{1,0:T(8,128)} async-done(((f32[512,1024]{1,0:T(8,128)}), f32[32,1024]{1,0:T(8,128)}) %reduce-scatter.7.cloned.1.call-update) | async-done | bytes 131088
  311.1 1.1 copy.12
  314.3 1.3 pad_maximum_fusion
  315.7 1.3 fusion
  317.1 1.3 fusion.2
  318.4 1.3 convolution_bitcast_fusion.1
  319.7 1.3 convolution_bitcast_fusion.2
  321.0 1.0 broadcast_multiply_fusion
  322.1 1.9 copy.10
  323.9 113.0 %reduce-scatter.5.cloned.1.call-done = f32[48,256]{1,0:T(8,128)} async-done(((f32[1536,256]{1,0:T(8,128)}), f32[48,256]{1,0:T(8,128)}) %reduce-scatter.5.cloned.1.call-update) | async-done | bytes 49168 | tf_op jit(solution)/shard_map/reduce_scatter | solution.py:34
  437.0 44.9 %all-gather = f32[768,256]{1,0:T(8,128)S(1)} all-gather(f32[48,256]{1,0:T(8,128)} %reduce-scatter.5.cloned.1.call-done), channel_id=2, replica_groups=mesh['grp'=16,'blk'=32] {'grp'}, dimensions={0}, use_global_device_ids=true | all-gather | bytes 835584 | tf_op jit(solution)/shard_map/all_gather | solution.py:9
  481.9 0.6 fusion.32
  482.5 1.5 slice_add_fusion
  (34 shorter events, 2.6 us)
Async XLA Ops:
  7.2 79.8 %copy-start = (f32[1024,512]{1,0:T(8,128)S(1)}, f32[1024,512]{1,0:T(8,128)}, u32[]{:S(2)}) copy-start(f32[1024,512]{1,0:T(8,128)} %param.6) | copy-start | bytes 6291460
  7.2 79.8 %all-gather.3.cloned.1.call-start = ((), (), s32[]{:S(2)}) async-start(), calls=%async_computation.2 | async-start | bytes 4325376 | tf_op jit(solution)/shard_map/all_gather | solution.py:26
  13.2 297.9 %reduce-scatter.7.cloned.1.call-start = ((), (), s32[]{:S(2)}) async-start(), calls=%async_computation.4 | async-start | bytes 2228224
  96.9 0.9 copy-start.4
  96.9 340.0 %reduce-scatter.5.cloned.1.call-start = ((), (), s32[]{:S(2)}) async-start(), calls=%async_computation.3 | async-start | bytes 1622016 | tf_op jit(solution)/shard_map/reduce_scatter | solution.py:34
  97.8 214.3 %collective-permute-start = (f32[32,1024]{1,0:T(8,128)S(1)}, f32[32,1024]{1,0:T(8,128)S(1)}, u32[]{:S(2)}, u32[]{:S(2)}) collective-permute-start(f32[32,1024]{1,0:T(8,128)S(1)} %copy-done.4), channel_id=1, source_target_pairs={{0,0},{1,32},{2,64},{3,96},{4,128},{5,160},{6,192},{7,224},{8,256}... | collective-permute-start | bytes 393224 | tf_op jit(solution)/shard_map/ppermute | solution.py:47
  314.3 1.5 copy-start.1
  318.4 1.3 copy-start.2
  321.0 160.9 %copy-start.3 = (f32[256,256]{1,0:T(8,128)S(1)}, f32[256,256]{1,0:T(8,128)}, u32[]{:S(2)}) copy-start(f32[256,256]{1,0:T(8,128)} %copy-done.2) | copy-start | bytes 786436
Sparse Core Ops, SparseCore 0:
  13.3 73.6 all-gather.2
  97.1 213.9 reduce-scatter.6
  315.7 121.2 reduce-scatter.4
